TPU v7x, 128 devices: a whole 4x4x4 slice. The times are simulated.
128 devices in a mesh: section: 8 (over x, z_hi), ctx: 16 (over z_lo, y, core).
Axes of the slice: x: 4, y: 4, z: 4 (z_hi: 2, z_lo: 2; z = z_hi * 2 + z_lo), core: 2. Of those that a mesh axis runs over, the one named last changes fastest.
Arguments:
- acts: bfloat16 [8, 2048, 12288], P('section', 'ctx'), may hold values from -6 to 6
- cots: bfloat16 [8, 2048, 4096], P('section', 'ctx'), may hold values from -1.1953125 to 1.1953125
- kern: float32 [8, 7, 12288], P('section'), may hold values from -2 to 2
- filt: bfloat16 [8, 4096, 2048], P('section', 'ctx'), may hold values from -9 to 9
- skip: float32 [8, 4096], P('section'), may hold values from 0.5 to 1.5
Outputs:
- output: bfloat16 [8, 2048, 4096], P('section', 'ctx')
- input_grad: bfloat16 [8, 2048, 12288], P('section', 'ctx')
- kern_grad: float32 [8, 7, 12288], P('section')
- filt_grad: float32 [8, 4096, 2048], P('section', 'ctx')
- skip_grad: float32 [8, 4096], P('section', 'ctx')
All inputs are finite; a program needn't handle non-finite values.
Results may differ from a plain program's by a relative error of at most 0.023.
Values may be sent and summed in bfloat16 or wider, within the bound.
No kernel may reach another device: no remote copies, remote signals or barrier semaphores. Data moves between devices by JAX's collectives and lax.ppermute only.
A program may use at most 192 MiB of HBM per device.

v0:
```python
import math
import jax
import jax.numpy as jnp
from jax import lax
from jax.sharding import PartitionSpec as P


def passed_along(value, axis, steps):
    count = lax.axis_size(axis)
    pairs = [(source, (source + steps) % count) for source in range(count)]
    return lax.ppermute(value, axis, pairs)


def from_behind(block, axis, distance):
    devices = range(lax.axis_size(axis))
    route = [(i - distance, i) for i in devices if i - distance in devices]
    return lax.ppermute(block, axis, route)


def factor_length(total):
    best = 2
    for divisor in range(2, math.isqrt(total) + 1):
        if total % divisor == 0 and divisor % 2 == 0:
            best = divisor
    return (best, total // best)


def phases(rows, cols, total):
    left = jnp.arange(rows, dtype=jnp.int32)[:, None]
    right = jnp.arange(cols, dtype=jnp.int32)[None, :]
    return (left * right % total).astype(jnp.float32) * (2.0 * math.pi / total)


def block_table(cos_t, sin_t, sign):
    top = jnp.stack([cos_t, sign * sin_t], axis=1)
    bottom = jnp.stack([-sign * sin_t, cos_t], axis=1)
    return jnp.stack([top, bottom], axis=0)


def make_tables(first, second):
    total = first * second
    outer = phases(first, first // 2, first)
    twist = phases(first, second, total)
    inner = phases(second, second, second)
    outer_pair = jnp.stack([jnp.cos(outer), -jnp.sin(outer)], axis=0)
    inner_cos = jnp.cos(inner)
    inner_sin = jnp.sin(inner)
    return (
        outer_pair,
        jnp.cos(twist),
        jnp.sin(twist),
        block_table(inner_cos, inner_sin, 1.0),
        block_table(inner_cos, inner_sin, -1.0),
    )


def contract(form, table, values):
    return jnp.einsum(form, table, values, precision=lax.Precision.HIGH)


def contract_narrow(form, table, values):
    upper = table.astype(jnp.bfloat16)
    lower = (table - upper.astype(jnp.float32)).astype(jnp.bfloat16)
    return jnp.einsum(form, upper, values, preferred_element_type=jnp.float32) + jnp.einsum(
        form, lower, values, preferred_element_type=jnp.float32
    )


def forward_transform(signal, tables):
    outer_pair, twist_cos, twist_sin, inner_fwd, inner_inv = tables
    first, second = twist_cos.shape
    columns = signal.shape[1]
    blocked = signal.reshape(first // 2, second, columns)
    spread = contract_narrow("pkm,mjc->pkjc", outer_pair, blocked)
    a_real = spread[0]
    a_imag = spread[1]
    b_real = a_real * twist_cos[:, :, None] + a_imag * twist_sin[:, :, None]
    b_imag = a_imag * twist_cos[:, :, None] - a_real * twist_sin[:, :, None]
    stacked = jnp.stack([b_real, b_imag], axis=0)
    return contract("pqsj,skjc->pkqc", inner_fwd, stacked)


def cmul(left, right, conj_right):
    if conj_right:
        return jnp.stack(
            [left[0] * right[0] + left[1] * right[1], left[1] * right[0] - left[0] * right[1]],
            axis=0,
        )
    return jnp.stack(
        [left[0] * right[0] - left[1] * right[1], left[0] * right[1] + left[1] * right[0]], axis=0
    )


def inverse_transform(spectrum, tables):
    outer_pair, twist_cos, twist_sin, inner_fwd, inner_inv = tables
    first, second = twist_cos.shape
    columns = spectrum.shape[3]
    back = contract("pjsq,skqc->pkjc", inner_inv, spectrum)
    g_real = back[0] * twist_cos[:, :, None] - back[1] * twist_sin[:, :, None]
    g_imag = back[0] * twist_sin[:, :, None] + back[1] * twist_cos[:, :, None]
    result = contract("skm,skjc->mjc", outer_pair, jnp.stack([g_real, g_imag], axis=0))
    return result.reshape(first // 2 * second, columns) / (first * second)


def on_device(acts, cots, kern, filt, skip):
    source = passed_along(acts, "section", 1)[0]
    incoming = passed_along(cots, "section", -1)[0]
    taps = kern.shape[1]
    margin = taps - 1
    tokens_dev, feats = source.shape
    width = feats // 3
    groups = lax.axis_size("ctx")
    chans = width // groups
    seq_len = tokens_dev * groups
    before = from_behind(source[tokens_dev - margin :], "ctx", 1)
    padded = jnp.concatenate([before, source], axis=0).astype(jnp.float32)
    weights = kern[0]
    feature = sum(
        (
            weights[offset][None, :] * padded[margin - offset : margin - offset + tokens_dev]
            for offset in range(taps)
        )
    )
    query = feature[:, :width]
    keyed = feature[:, width : 2 * width]
    value = feature[:, 2 * width :]
    gated = (keyed * value).astype(jnp.bfloat16)
    gain_all = skip[0]
    gain_part = lax.dynamic_slice_in_dim(gain_all, lax.axis_index("ctx") * chans, chans)
    first, second = factor_length(2 * seq_len)
    tables = make_tables(first, second)
    filt_spec = forward_transform(filt[0].T, tables)
    grad_in = incoming.astype(jnp.float32)
    grad_mix = (grad_in * query).astype(jnp.bfloat16)
    gated_part = lax.all_to_all(gated, "ctx", split_axis=1, concat_axis=0, tiled=True)
    gated_f = gated_part.astype(jnp.float32)
    gated_spec = forward_transform(gated_part, tables)
    mixed = inverse_transform(cmul(gated_spec, filt_spec, False), tables)
    mixed_part = mixed.astype(jnp.bfloat16)
    mixed_seq = lax.all_to_all(mixed_part, "ctx", split_axis=0, concat_axis=1, tiled=True)
    grad_part = lax.all_to_all(grad_mix, "ctx", split_axis=1, concat_axis=0, tiled=True)
    gated_f, gated_spec = (gated_f, gated_spec)
    grad_f = grad_part.astype(jnp.float32)
    grad_spec = forward_transform(grad_part, tables)
    back = inverse_transform(cmul(grad_spec, filt_spec, True), tables)
    filt_grad = inverse_transform(cmul(grad_spec, gated_spec, True), tables)
    through = (back + gain_part[None, :] * grad_f).astype(jnp.bfloat16)
    skip_grad = jnp.sum(grad_f * gated_f, axis=0)
    through_part, filt_grad, skip_grad = (through, filt_grad, skip_grad)
    through_seq = lax.all_to_all(through_part, "ctx", split_axis=0, concat_axis=1, tiled=True)
    inner = mixed_seq.astype(jnp.float32) + gain_all[None, :] * gated.astype(jnp.float32)
    output = (query * inner).astype(jnp.bfloat16)
    through_f = through_seq.astype(jnp.float32)
    feat_grad = jnp.concatenate([grad_in * inner, through_f * value, through_f * keyed], axis=1)
    after = from_behind(feat_grad[:margin].astype(jnp.bfloat16), "ctx", -1).astype(jnp.float32)
    extended = jnp.concatenate([feat_grad, after], axis=0)
    input_grad = sum(
        (
            weights[offset][None, :] * extended[offset : offset + tokens_dev]
            for offset in range(taps)
        )
    ).astype(jnp.bfloat16)
    partial_kern = jnp.sum(
        jnp.stack(
            [
                feat_grad * padded[margin - offset : margin - offset + tokens_dev]
                for offset in range(taps)
            ],
            axis=0,
        ),
        axis=1,
    )
    kern_grad = lax.psum(partial_kern.astype(jnp.bfloat16), "ctx").astype(jnp.float32)
    return (output[None], input_grad[None], kern_grad[None], filt_grad.T[None], skip_grad[None])


def solution(mesh):
    return jax.shard_map(
        on_device,
        mesh=mesh,
        in_specs=(
            P("section", "ctx", None),
            P("section", "ctx", None),
            P("section", None, None),
            P("section", "ctx", None),
            P("section", None),
        ),
        out_specs=(
            P("section", "ctx", None),
            P("section", "ctx", None),
            P("section", None, None),
            P("section", "ctx", None),
            P("section", "ctx"),
        ),
        check_vma=False,
    )
```

profile of v0, /device:TPU:25, one launch (start us, length us, event | category | flops | bytes accessed | tf_op | source)
XLA Modules:
  0.0 614.9 jit_solution(2262165847482371102)
XLA Ops:
  7.2 2.3 copy.84
  9.5 5.8 collective-permute-start.2
  15.3 4.6 copy.69
  22.4 82.2 %collective-permute-done = bf16[1,128,12288]{1,2,0:T(8,128)(2,1)} collective-permute-done((bf16[1,128,12288]{1,2,0:T(8,128)(2,1)}, bf16[1,128,12288]{1,2,0:T(8,128)(2,1)}, u32[]{:S(2)}, u32[]{:S(2)}) %collective-permute-start) | collective-permute-done | bytes 3145760 | tf_op jit(solution)/shard_map/ppermute | solution.py:11
  104.6 3.6 slice_bitcast_fusion
  108.2 3.9 copy.70
  112.0 2.7 collective-permute-start.1
  117.6 3.6 copy.71
  121.3 4.7 maximum_convert_fusion
  126.1 24.5 %multiply_add_fusion = f32[128,12288]{0,1:T(8,128)} fusion(f32[134,12288]{0,1:T(8,128)S(1)} %maximum_convert_fusion, f32[12288]{0:T(1024)S(1)} %bitcast.243, f32[12288]{0:T(1024)S(1)} %bitcast.245, f32[12288]{0:T(1024)S(1)} %bitcast.235, f32[12288]{0:T(1024)S(1)} %bitcast.237, f32[12288]{0:T(1024)S(1)} %bitcast.239, f32[12288]{0:T(1024)S(1)} %bitcast.241, ...), kind=kLoop, calls=%fused_computation.60 | loop fusion | flops 20447232 | bytes 50675712 | tf_op jit(solution)/shard_map/add | solution.py:118
  150.6 3.1 fusion.50
  153.8 7.0 %all-to-all-start.2 = ((bf16[128,16,256]{0,2,1:T(8,128)(2,1)}), bf16[128,16,256]{0,2,1:T(8,128)(2,1)S(1)}, u32[]{:S(2)}, u32[]{:S(2)}) async-start(bf16[128,16,256]{0,2,1:T(8,128)(2,1)} %bitcast.232), calls=%async_computation.2 | async-start | bytes 2097152 | tf_op jit(solution)/shard_map/all_to_all | solution.py:141
  162.1 4.6 convolution_add_fusion.1
  166.7 7.9 %all-to-all-done.2 = bf16[128,16,256]{0,2,1:T(8,128)(2,1)S(1)} async-done(((bf16[128,16,256]{0,2,1:T(8,128)(2,1)}), bf16[128,16,256]{0,2,1:T(8,128)(2,1)S(1)}, u32[]{:S(2)}, u32[]{:S(2)}) %all-to-all-start.2) | async-done | bytes 1048608 | tf_op jit(solution)/shard_map/all_to_all | solution.py:141
  178.8 7.3 %multiply_add_fusion.5 = (f32[1,64,64,256]{3,1,2,0:T(8,128)}, f32[1,64,64,256]{3,1,2,0:T(8,128)}, f32[1,64,64,256]{3,1,2,0:T(8,128)}, f32[1,64,64,256]{3,1,2,0:T(8,128)}) fusion(f32[2,64,64,256]{3,1,2,0:T(8,128)S(1)} %convolution_add_fusion, f32[64,64]{0,1:T(8,128)S(1)} %get-tuple-element.64, f32[64,64]{0,1:T(8,128)S(1)} %get-tuple-element.65, ...), kind=kLoop, calls=%fused_computation.70 | loop fusion | flops 12582912 | bytes 33587200 | tf_op jit(solution)/shard_map/add | solution.py:77
  186.1 4.1 maximum_bitcast_fusion.4
  190.2 4.1 maximum_bitcast_fusion.1
  194.3 8.5 %fusion.40 = f32[2,64,64,256]{3,2,0,1:T(8,128)S(1)} fusion(f32[2,64,64,256,1]{3,1,2,0,4:T(8,128)S(1)} %maximum_bitcast_fusion.4, f32[1,64,2,64]{3,1,2,0:T(8,128)S(1)} %get-tuple-element.57, f32[1,64,2,64]{3,1,2,0:T(8,128)S(1)} %get-tuple-element.60), kind=kOutput, calls=%fused_computation.84 | convolution fusion | flops 1610629120 | bytes 16842752 | tf_op jit(solution)/shard_map/pqsj,skjc->pkqc/dot_general | solution.py:58
  202.8 8.7 %fusion.37 = f32[2,64,64,256]{3,2,0,1:T(8,128)S(1)} fusion(f32[2,64,64,256,1]{3,1,2,0,4:T(8,128)S(1)} %maximum_bitcast_fusion.1, f32[1,64,2,64]{3,1,2,0:T(8,128)S(1)} %get-tuple-element.57, f32[1,64,2,64]{3,1,2,0:T(8,128)S(1)} %get-tuple-element.60), kind=kOutput, calls=%fused_computation.83 | convolution fusion | flops 1610629120 | bytes 16842752 | tf_op jit(solution)/shard_map/pqsj,skjc->pkqc/dot_general | solution.py:58
  211.5 4.7 multiply_add_fusion.4
  217.3 6.5 %fusion.44 = f32[64,256,2,64]{1,3,2,0:T(8,128)S(1)} fusion(f32[1,64,64,256]{3,2,0,1:T(8,128)} %get-tuple-element.23, f32[1,64,64,256]{3,2,0,1:T(8,128)} %get-tuple-element.22, f32[1,64,2,64]{3,1,2,0:T(8,128)S(1)} %get-tuple-element.61, f32[1,64,2,64]{3,1,2,0:T(8,128)S(1)} %get-tuple-element.56), kind=kOutput, calls=%fused_computation.86 | convolution fusion | flops 1612726272 | bytes 16842752 | tf_op jit(solution)/shard_map/pjsq,skqc->pkjc/dot_general | solution.py:58
  223.7 4.9 copy.164
  230.1 3.0 bitcast_multiply_fusion.1
  233.1 2.5 copy.91
  235.6 1.9 copy.92
  238.0 19.4 %all_to_all.52 = bf16[16,128,256]{1,2,0:T(8,128)(2,1)S(1)} all-to-all(bf16[16,128,256]{1,2,0:T(8,128)(2,1)S(1)} %fusion.48), channel_id=1, replica_groups=mesh['section'=8,'ctx'=16] {'ctx'}, dimensions={0} | all-to-all | bytes 2097152 | tf_op jit(solution)/shard_map/all_to_all | solution.py:150
  257.4 4.0 bitcast_multiply_fusion.4
  262.3 20.2 %all_to_all.53 = bf16[128,16,256]{0,2,1:T(8,128)(2,1)} all-to-all(bf16[128,16,256]{0,2,1:T(8,128)(2,1)S(1)} %bitcast.220), channel_id=1, replica_groups=mesh['section'=8,'ctx'=16] {'ctx'}, dimensions={1} | all-to-all | bytes 2097152 | tf_op jit(solution)/shard_map/all_to_all | solution.py:135
  282.5 2.3 copy.72
  284.7 2.6 fusion.65
  290.1 4.2 maximum_bitcast_fusion
  294.3 14.0 %fusion.34 = f32[2,64,64,256]{3,2,0,1:T(8,128)} fusion(f32[2,64,64,256,1]{3,1,2,0,4:T(8,128)} %maximum_bitcast_fusion, f32[1,64,2,64]{3,1,2,0:T(8,128)S(1)} %get-tuple-element.57, f32[1,64,2,64]{3,1,2,0:T(8,128)S(1)} %get-tuple-element.60), kind=kOutput, calls=%fused_computation.82 | convolution fusion | flops 1610629120 | bytes 16842752 | tf_op jit(solution)/shard_map/pqsj,skjc->pkqc/dot_general | solution.py:58
  308.3 11.9 %multiply_add_fusion.2 = (f32[1,64,64,256]{3,2,0,1:T(8,128)}, f32[1,64,64,256]{3,2,0,1:T(8,128)}, f32[1,64,64,256]{3,2,0,1:T(8,128)}, f32[1,64,64,256]{3,2,0,1:T(8,128)}) fusion(f32[2,64,64,256]{3,2,0,1:T(8,128)S(1)} %bitcast.212, f32[2,64,64,256]{3,2,0,1:T(8,128)} %fusion.34, f32[2,64,64,256]{3,2,0,1:T(8,128)} %copy-done.8), kind=kLoop, calls=%fused_computation.64 | loop fusion | flops 12582912 | bytes 41943040 | tf_op jit(solution)/shard_map/add | solution.py:86
  320.1 6.4 %fusion.45 = f32[64,256,2,64]{1,3,2,0:T(8,128)S(1)} fusion(f32[1,64,64,256]{3,2,0,1:T(8,128)} %get-tuple-element.38, f32[1,64,64,256]{3,2,0,1:T(8,128)} %get-tuple-element.39, f32[1,64,2,64]{3,1,2,0:T(8,128)S(1)} %get-tuple-element.61, f32[1,64,2,64]{3,1,2,0:T(8,128)S(1)} %get-tuple-element.56), kind=kOutput, calls=%fused_computation.87 | convolution fusion | flops 1612726272 | bytes 16842752 | tf_op jit(solution)/shard_map/pjsq,skqc->pkjc/dot_general | solution.py:58
  326.6 4.9 copy.165
  331.4 6.5 %fusion.43 = f32[64,256,2,64]{1,3,2,0:T(8,128)S(1)} fusion(f32[1,64,64,256]{3,2,0,1:T(8,128)} %get-tuple-element.21, f32[1,64,64,256]{3,2,0,1:T(8,128)} %get-tuple-element.20, f32[1,64,2,64]{3,1,2,0:T(8,128)S(1)} %get-tuple-element.61, f32[1,64,2,64]{3,1,2,0:T(8,128)S(1)} %get-tuple-element.56), kind=kOutput, calls=%fused_computation.85 | convolution fusion | flops 1612726272 | bytes 16842752 | tf_op jit(solution)/shard_map/pjsq,skqc->pkjc/dot_general | solution.py:58
  337.9 8.2 %copy.163 = f32[64,256,2,64]{1,0,3,2:T(8,128)} copy(f32[64,256,2,64]{1,3,2,0:T(8,128)S(1)} %fusion.43) | data formatting | bytes 16777216 | tf_op jit(solution)/shard_map/pjsq,skqc->pkjc/dot_general | solution.py:58
  346.1 7.9 %multiply_subtract_fusion = (f32[1,64,64,256]{3,1,2,0:T(8,128)}, f32[1,64,64,256]{3,1,2,0:T(8,128)}, f32[1,64,64,256]{3,1,2,0:T(8,128)S(1)}, f32[1,64,64,256]{3,1,2,0:T(8,128)}) fusion(f32[2,64,64,256]{3,1,2,0:T(8,128)} %bitcast.217, f32[64,64]{0,1:T(8,128)S(1)} %get-tuple-element.64, f32[64,64]{0,1:T(8,128)S(1)} %get-tuple-element.65, ...), kind=kLoop, calls=%fused_computation.62 | loop fusion | flops 12582912 | bytes 33587200 | tf_op jit(solution)/shard_map/sub | solution.py:99
  353.9 5.1 fusion.51
  360.6 6.6 %all-to-all-start.1 = ((bf16[16,128,256]{2,1,0:T(8,128)(2,1)}), bf16[16,128,256]{2,1,0:T(8,128)(2,1)}, u32[]{:S(2)}, u32[]{:S(2)}) async-start(bf16[16,128,256]{2,1,0:T(8,128)(2,1)} %bitcast.231), calls=%async_computation.1 | async-start | bytes 2097152 | tf_op jit(solution)/shard_map/all_to_all | solution.py:140
  367.3 5.3 bitcast_multiply_fusion
  372.6 2.5 copy.97
  375.1 2.9 copy.100
  378.0 2.1 fusion.49
  381.2 2.8 convert_bitcast_fusion
  384.0 2.9 copy.83
  386.9 3.8 convert_multiply_fusion.1
  390.7 6.7 %pad_maximum_fusion.1 = bf16[128,12288]{0,1:T(8,128)(2,1)} fusion(f32[128,4096]{0,1:T(8,128)S(1)} %copy-done.1, f32[128,4096]{0,1:T(8,128)S(1)} %get-tuple-element.40, f32[128,4096]{0,1:T(8,128)S(1)} %get-tuple-element.43), kind=kLoop, calls=%fused_computation.52 | loop fusion | flops 9437184 | bytes 9437184 | tf_op jit(solution)/shard_map/concatenate | solution.py:154
  397.4 10.1 %bitcast_dynamic-update-slice_fusion.6 = f32[7,128,12288]{1,2,0:T(8,128)} fusion(f32[134,12288]{0,1:T(8,128)} %copy-done, f32[128,4096]{0,1:T(8,128)S(1)} %copy-done.1, f32[128,4096]{0,1:T(8,128)S(1)} %get-tuple-element.40, f32[128,4096]{0,1:T(8,128)S(1)} %get-tuple-element.43), kind=kLoop, calls=%fused_computation.59 | loop fusion | flops 4718591 | bytes 18874368
  407.5 3.2 copy.93
  410.7 2.2 collective-permute-start.3
  412.9 10.0 %bitcast_dynamic-update-slice_fusion.5 = f32[7,128,12288]{1,2,0:T(8,128)} fusion(f32[7,128,12288]{1,2,0:T(8,128)} %bitcast_dynamic-update-slice_fusion.6, f32[134,12288]{0,1:T(8,128)} %copy-done, f32[128,4096]{0,1:T(8,128)} %get-tuple-element.41, f32[128,4096]{0,1:T(8,128)S(1)} %get-tuple-element.40, f32[128,4096]{0,1:T(8,128)} %copy-done.4), kind=kLoop, calls=%fused_computation.58 | loop fusion | flops 4718592 | bytes 18874368
  422.9 10.3 %bitcast_dynamic-update-slice_fusion.4 = f32[7,128,12288]{1,2,0:T(8,128)} fusion(f32[7,128,12288]{1,2,0:T(8,128)} %bitcast_dynamic-update-slice_fusion.5, f32[134,12288]{0,1:T(8,128)} %copy-done, f32[128,4096]{0,1:T(8,128)S(1)} %copy-done.2, f32[128,4096]{0,1:T(8,128)S(1)} %get-tuple-element.40, f32[128,4096]{0,1:T(8,128)S(1)} %copy-done.5), kind=kLoop, calls=%fused_computation.57 | loop fusion | flops 4718592 | bytes 18874368
  433.2 7.4 %bitcast_dynamic-update-slice_fusion.3 = f32[7,128,12288]{1,2,0:T(8,128)} fusion(f32[7,128,12288]{1,2,0:T(8,128)} %bitcast_dynamic-update-slice_fusion.4, f32[134,12288]{0,1:T(8,128)S(1)} %bitcast.210, f32[128,4096]{0,1:T(8,128)S(1)} %copy-done.2, f32[128,4096]{0,1:T(8,128)S(1)} %get-tuple-element.40, f32[128,4096]{0,1:T(8,128)S(1)} %copy-done.5), kind=kLoop, calls=%fused_computation.56 | loop fusion | flops 4718592 | bytes 18874368
  440.6 7.3 %bitcast_dynamic-update-slice_fusion.2 = f32[7,128,12288]{1,2,0:T(8,128)} fusion(f32[7,128,12288]{1,2,0:T(8,128)} %bitcast_dynamic-update-slice_fusion.3, f32[134,12288]{0,1:T(8,128)S(1)} %bitcast.210, f32[128,4096]{0,1:T(8,128)S(1)} %copy-done.2, f32[128,4096]{0,1:T(8,128)S(1)} %get-tuple-element.40, f32[128,4096]{0,1:T(8,128)S(1)} %copy-done.5), kind=kLoop, calls=%fused_computation.55 | loop fusion | flops 4718592 | bytes 18874368
  447.8 7.6 %bitcast_dynamic-update-slice_fusion.1 = f32[7,128,12288]{1,2,0:T(8,128)} fusion(f32[7,128,12288]{1,2,0:T(8,128)} %bitcast_dynamic-update-slice_fusion.2, f32[134,12288]{0,1:T(8,128)S(1)} %bitcast.210, f32[128,4096]{0,1:T(8,128)S(1)} %copy-done.2, f32[128,4096]{0,1:T(8,128)S(1)} %get-tuple-element.40, f32[128,4096]{0,1:T(8,128)S(1)} %copy-done.5), kind=kLoop, calls=%fused_computation.54 | loop fusion | flops 4718592 | bytes 18874368
  455.4 7.2 %bitcast_dynamic-update-slice_fusion = f32[7,128,12288]{1,2,0:T(8,128)} fusion(f32[7,128,12288]{1,2,0:T(8,128)} %bitcast_dynamic-update-slice_fusion.1, f32[134,12288]{0,1:T(8,128)S(1)} %bitcast.210, f32[128,4096]{0,1:T(8,128)S(1)} %copy-done.2, f32[128,4096]{0,1:T(8,128)S(1)} %get-tuple-element.40, f32[128,4096]{0,1:T(8,128)S(1)} %copy-done.5), kind=kLoop, calls=%fused_computation.53 | loop fusion | flops 4718592 | bytes 18874368 | tf_op jit(solution)/shard_map/stack | solution.py:164
  463.9 20.5 %reduce_sum.18 = bf16[7,12288]{1,0:T(8,128)(2,1)S(1)} reduce(f32[7,128,12288]{1,2,0:T(8,128)} %bitcast_dynamic-update-slice_fusion, f32[]{:T(128)} %constant.55.clone.1), dimensions={1}, to_apply=%region_0.1 | reduce | flops 10924032 | bytes 44212228 | tf_op jit(solution)/shard_map/reduce_sum | solution.py:163
  485.4 3.5 copy.94
  489.0 12.3 %pad_maximum_fusion = f32[134,12288]{0,1:T(8,128)} fusion(f32[6,12288]{0,1:T(8,128)} %copy.94, f32[128,4096]{0,1:T(8,128)} %get-tuple-element.41, f32[128,4096]{0,1:T(8,128)S(1)} %get-tuple-element.40, f32[128,4096]{0,1:T(8,128)} %copy-done.4), kind=kLoop, calls=%fused_computation | loop fusion | flops 4939776 | bytes 13172736 | tf_op jit(solution)/shard_map/concatenate | solution.py:156
  501.3 31.6 %fusion.46 = bf16[1,128,12288]{1,2,0:T(8,128)(2,1)} fusion(f32[134,12288]{0,1:T(8,128)} %pad_maximum_fusion, f32[12288]{0:T(1024)S(1)} %bitcast.244, f32[12288]{0:T(1024)S(1)} %bitcast.246, f32[12288]{0:T(1024)S(1)} %bitcast.236, f32[12288]{0:T(1024)S(1)} %bitcast.238, f32[12288]{0:T(1024)S(1)} %bitcast.240, f32[12288]{0:T(1024)S(1)} %bitcast.242, ...), kind=kLoop, calls=%fused_computation.89 | loop fusion | flops 25165824 | bytes 47529984 | tf_op jit(solution)/shard_map/broadcast_in_dim | solution.py:174
  532.9 4.6 copy.99
  537.5 68.2 %all-reduce.2.cloned.1.call-done = bf16[1,7,12288]{2,0,1:T(2,128)(2,1)} async-done(((bf16[1,7,12288]{2,0,1:T(2,128)(2,1)}), bf16[1,7,12288]{2,0,1:T(2,128)(2,1)}) %all-reduce.2.cloned.1.call-update) | async-done | bytes 172048 | tf_op jit(solution)/shard_map/psum | solution.py:173
  605.8 2.1 broadcast_in_dim.16
  (107 shorter events, 22.5 us)
Async XLA Ops:
  7.2 14.5 %copy-start.29 = (f32[1,7,12288]{2,0,1:T(1,128)S(1)}, f32[1,7,12288]{2,0,1:T(1,128)}, u32[]{:S(2)}) copy-start(f32[1,7,12288]{2,0,1:T(1,128)} %param.7) | copy-start | bytes 1032196
  9.5 141.1 %collective-permute-start.2 = (bf16[1,128,4096]{1,2,0:T(8,128)(2,1)}, bf16[1,128,4096]{1,2,0:T(8,128)(2,1)S(1)}, u32[]{:S(2)}, u32[]{:S(2)}) collective-permute-start(bf16[1,128,4096]{1,2,0:T(8,128)(2,1)} %copy.84), channel_id=1, source_target_pairs={{0,112},{16,0},{32,16},{48,32},{64,48},{80,64},{96,80},{112,96},{1... | collective-permute-start | bytes 3145736 | tf_op jit(solution)/shard_map/ppermute | solution.py:11
  19.9 96.0 %copy-start.14 = (bf16[1,256,2048]{2,1,0:T(8,128)(2,1)S(1)}, bf16[1,256,2048]{2,1,0:T(8,128)(2,1)}, u32[]{:S(2)}) copy-start(bf16[1,256,2048]{2,1,0:T(8,128)(2,1)} %param.8) | copy-start | bytes 3145732
  19.9 84.7 %collective-permute-start = (bf16[1,128,12288]{1,2,0:T(8,128)(2,1)}, bf16[1,128,12288]{1,2,0:T(8,128)(2,1)}, u32[]{:S(2)}, u32[]{:S(2)}) collective-permute-start(bf16[1,128,12288]{1,2,0:T(8,128)(2,1)} %copy.69), channel_id=1, source_target_pairs={{0,16},{16,32},{32,48},{48,64},{64,80},{80,96},{96,112},{112,0},{1... | collective-permute-start | bytes 9437192 | tf_op jit(solution)/shard_map/ppermute | solution.py:11
  22.4 103.6 %copy-start.15 = (f32[1,1,12288]{2,0,1:T(1,128)}, f32[1,1,12288]{2,0,1:T(1,128)S(1)}, u32[]{:S(2)}) copy-start(f32[1,1,12288]{2,0,1:T(1,128)S(1)} %get-tuple-element.45) | copy-start | bytes 147460
  112.0 5.6 collective-permute-start.1
  121.2 4.8 copy-start.17
  121.2 4.8 copy-start.19
  121.2 4.8 copy-start.21
  121.2 4.8 copy-start.23
  121.2 4.8 copy-start.25
  121.2 4.8 copy-start.27
  126.0 24.6 %copy-start = (f32[134,12288]{0,1:T(8,128)}, f32[134,12288]{0,1:T(8,128)S(1)}, u32[]{:S(2)}) copy-start(f32[134,12288]{0,1:T(8,128)S(1)} %maximum_convert_fusion) | copy-start | bytes 19759108
  150.6 11.4 %copy-start.13 = (bf16[1,128,4096]{1,2,0:T(8,128)(2,1)}, bf16[1,128,4096]{1,2,0:T(8,128)(2,1)S(1)}, u32[]{:S(2)}) copy-start(bf16[1,128,4096]{1,2,0:T(8,128)(2,1)S(1)} %collective-permute-done.2) | copy-start | bytes 3145732
  153.8 20.8 %all-to-all-start.2 = ((bf16[128,16,256]{0,2,1:T(8,128)(2,1)}), bf16[128,16,256]{0,2,1:T(8,128)(2,1)S(1)}, u32[]{:S(2)}, u32[]{:S(2)}) async-start(bf16[128,16,256]{0,2,1:T(8,128)(2,1)} %bitcast.232), calls=%async_computation.2 | async-start | bytes 2097152 | tf_op jit(solution)/shard_map/all_to_all | solution.py:141
  175.1 2.6 slice-start.5
  176.4 2.4 slice-start.6
  202.8 8.7 %copy-start.7 = (f32[2,64,64,256]{3,2,0,1:T(8,128)}, f32[2,64,64,256]{3,2,0,1:T(8,128)S(1)}, u32[]{:S(2)}) copy-start(f32[2,64,64,256]{3,2,0,1:T(8,128)S(1)} %fusion.40) | copy-start | bytes 25165828
  211.5 5.8 copy-start.8
  233.1 4.5 copy-start.31
  261.3 1.0 copy-start.9
  284.7 2.6 copy-start.11
  290.1 18.2 %slice-start.3 = ((s8[8388608]{0:T(1024)(128)(4,1)}), s8[4194304]{0:T(1024)(128)(4,1)S(1)}, s32[]{:S(2)}) async-start(s8[8388608]{0:T(1024)(128)(4,1)} %bitcast.211), calls=%async_computation.8 | async-start | bytes 8388608
  294.3 14.0 %slice-start.4 = ((s8[8388608]{0:T(1024)(128)(4,1)}), s8[4194304]{0:T(1024)(128)(4,1)S(1)}, s32[]{:S(2)}) async-start(s8[8388608]{0:T(1024)(128)(4,1)} %bitcast.211), calls=%async_computation.9 | async-start | bytes 8388608
  360.6 20.5 %all-to-all-start.1 = ((bf16[16,128,256]{2,1,0:T(8,128)(2,1)}), bf16[16,128,256]{2,1,0:T(8,128)(2,1)}, u32[]{:S(2)}, u32[]{:S(2)}) async-start(bf16[16,128,256]{2,1,0:T(8,128)(2,1)} %bitcast.231), calls=%async_computation.1 | async-start | bytes 2097152 | tf_op jit(solution)/shard_map/all_to_all | solution.py:140
  367.3 238.5 %all-reduce.2.cloned.1.call-start = ((), (), s32[]{:S(2)}) async-start(), calls=%async_computation.4 | async-start | bytes 688128 | tf_op jit(solution)/shard_map/psum | solution.py:173
  375.1 11.7 %copy-start.30 = (f32[1,4096]{1,0:T(1,128)S(1)}, f32[1,4096]{1,0:T(1,128)}, u32[]{:S(2)}) copy-start(f32[1,4096]{1,0:T(1,128)} %param.9) | copy-start | bytes 49156
  380.2 6.7 %copy-start.10 = (bf16[128,4096]{0,1:T(8,128)(2,1)S(1)}, bf16[128,4096]{0,1:T(8,128)(2,1)}, u32[]{:S(2)}) copy-start(bf16[128,4096]{0,1:T(8,128)(2,1)} %copy-done.9) | copy-start | bytes 3145732
  386.9 3.8 copy-start.1
  390.7 16.8 %copy-start.4 = (f32[128,4096]{0,1:T(8,128)}, f32[128,4096]{0,1:T(8,128)S(1)}, u32[]{:S(2)}) copy-start(f32[128,4096]{0,1:T(8,128)S(1)} %get-tuple-element.43) | copy-start | bytes 6291460
  410.7 12.2 %copy-start.2 = (f32[128,4096]{0,1:T(8,128)S(1)}, f32[128,4096]{0,1:T(8,128)}, u32[]{:S(2)}) copy-start(f32[128,4096]{0,1:T(8,128)} %get-tuple-element.41) | copy-start | bytes 6291460
  410.7 12.2 %copy-start.5 = (f32[128,4096]{0,1:T(8,128)S(1)}, f32[128,4096]{0,1:T(8,128)}, u32[]{:S(2)}) copy-start(f32[128,4096]{0,1:T(8,128)} %copy-done.4) | copy-start | bytes 6291460
  410.7 74.7 %collective-permute-start.3 = (bf16[6,12288]{1,0:T(8,128)(2,1)S(1)}, bf16[6,12288]{1,0:T(8,128)(2,1)S(1)}, u32[]{:S(2)}, u32[]{:S(2)}) collective-permute-start(bf16[6,12288]{1,0:T(8,128)(2,1)S(1)} %copy.93), channel_id=1, source_target_pairs={{1,0},{2,1},{3,2},{4,3},{5,4},{6,5},{7,6},{8,7},{9,8},{10,9},{11,1... | collective-permute-start | bytes 442376 | tf_op jit(solution)/shard_map/ppermute | solution.py:17
  412.9 20.3 %slice-start = ((s8[12582912]{0:T(1024)(128)(4,1)}), s8[4194304]{0:T(1024)(128)(4,1)S(1)}, s32[]{:S(2)}) async-start(s8[12582912]{0:T(1024)(128)(4,1)} %bitcast.209), calls=%async_computation.5 | async-start | bytes 8388608
  412.9 20.3 %slice-start.1 = ((s8[12582912]{0:T(1024)(128)(4,1)}), s8[4194304]{0:T(1024)(128)(4,1)S(1)}, s32[]{:S(2)}) async-start(s8[12582912]{0:T(1024)(128)(4,1)} %bitcast.209), calls=%async_computation.6 | async-start | bytes 8388608
  422.9 10.3 %slice-start.2 = ((s8[12582912]{0:T(1024)(128)(4,1)}), s8[4194304]{0:T(1024)(128)(4,1)S(1)}, s32[]{:S(2)}) async-start(s8[12582912]{0:T(1024)(128)(4,1)} %bitcast.209), calls=%async_computation.7 | async-start | bytes 8388608
  455.4 7.2 %copy-start.12 = (bf16[128,4096]{0,1:T(8,128)(2,1)S(1)}, bf16[128,4096]{0,1:T(8,128)(2,1)}, u32[]{:S(2)}) copy-start(bf16[128,4096]{0,1:T(8,128)(2,1)} %get-tuple-element.44) | copy-start | bytes 3145732
  488.9 12.3 %copy-start.3 = (f32[128,4096]{0,1:T(8,128)S(1)}, f32[128,4096]{0,1:T(8,128)}, u32[]{:S(2)}) copy-start(f32[128,4096]{0,1:T(8,128)} %get-tuple-element.41) | copy-start | bytes 6291460
  488.9 12.3 %copy-start.6 = (f32[128,4096]{0,1:T(8,128)S(1)}, f32[128,4096]{0,1:T(8,128)}, u32[]{:S(2)}) copy-start(f32[128,4096]{0,1:T(8,128)} %copy-done.4) | copy-start | bytes 6291460
  488.9 12.3 %copy-start.16 = (f32[1,1,12288]{2,0,1:T(1,128)S(1)}, f32[1,1,12288]{2,0,1:T(1,128)}, u32[]{:S(2)}) copy-start(f32[1,1,12288]{2,0,1:T(1,128)} %copy-done.15) | copy-start | bytes 147460
  488.9 12.3 %copy-start.18 = (f32[1,1,12288]{2,0,1:T(1,128)S(1)}, f32[1,1,12288]{2,0,1:T(1,128)}, u32[]{:S(2)}) copy-start(f32[1,1,12288]{2,0,1:T(1,128)} %get-tuple-element.46) | copy-start | bytes 147460
  488.9 12.3 %copy-start.20 = (f32[1,1,12288]{2,0,1:T(1,128)S(1)}, f32[1,1,12288]{2,0,1:T(1,128)}, u32[]{:S(2)}) copy-start(f32[1,1,12288]{2,0,1:T(1,128)} %get-tuple-element.47) | copy-start | bytes 147460
  488.9 12.3 %copy-start.22 = (f32[1,1,12288]{2,0,1:T(1,128)S(1)}, f32[1,1,12288]{2,0,1:T(1,128)}, u32[]{:S(2)}) copy-start(f32[1,1,12288]{2,0,1:T(1,128)} %get-tuple-element.48) | copy-start | bytes 147460
  488.9 12.3 %copy-start.24 = (f32[1,1,12288]{2,0,1:T(1,128)S(1)}, f32[1,1,12288]{2,0,1:T(1,128)}, u32[]{:S(2)}) copy-start(f32[1,1,12288]{2,0,1:T(1,128)} %get-tuple-element.49) | copy-start | bytes 147460
  488.9 12.3 %copy-start.26 = (f32[1,1,12288]{2,0,1:T(1,128)S(1)}, f32[1,1,12288]{2,0,1:T(1,128)}, u32[]{:S(2)}) copy-start(f32[1,1,12288]{2,0,1:T(1,128)} %get-tuple-element.50) | copy-start | bytes 147460
  488.9 12.3 %copy-start.28 = (f32[1,1,12288]{2,0,1:T(1,128)S(1)}, f32[1,1,12288]{2,0,1:T(1,128)}, u32[]{:S(2)}) copy-start(f32[1,1,12288]{2,0,1:T(1,128)} %get-tuple-element.51) | copy-start | bytes 147460
Sparse Core Ops, SparseCore 0:
  485.5 120.2 all-reduce.1
where the time goes:
time: 625 us; the launch traced here: 615 us
  other arithmetic  228 us (36%)
  waiting for transfers between devices  160 us (26%)
  matrix products  76.2 us (12%)
  local copies, waits for them, and re-layouts  72.4 us (12%)
  blocking collectives  39.5 us (6%)
  starting transfers between devices  24.3 us (4%)
  between operations  14.9 us (2%)
    ppermute x2, waiting for transfers between devices, passed_along(): return lax.ppermute(value, axis, pairs)  82.2 us
    psum x1, waiting for transfers between devices, on_device(): lax.psum(partial_kern.astype(jnp.bfloat16), 'ctx').astype(jnp.float32)  68.2 us
    dot_general x9, matrix products, contract(): return jnp.einsum(form, table, values, precision=lax.Precision.HIGH)  63.9 us
    unnamed x9, other arithmetic  52.6 us
    broadcast_in_dim x1, other arithmetic, on_device(): input_grad[None]  31.6 us
    add x1, other arithmetic, on_device(): sum((weights[offset][None, :] * padded[margin - offset:margin - offset +...  24.5 us
    reduce_sum x1, other arithmetic, on_device(): jnp.sum(jnp.stack([feat_grad * padded[margin - offset:margin - offset + t...  20.5 us
    all_to_all x1, blocking collectives, on_device(): lax.all_to_all(gated, 'ctx', split_axis=1, concat_axis=0, tiled=True)  20.2 us
  transfers between devices with their start and end apart: 7, of which 5 were waited for; matrix products, arithmetic and copies ran while one was open for 31% of the time, Pallas kernels for 0%

commit v1 on v0

--- a/solution.py
+++ b/solution.py
@@ -132,7 +132,10 @@
     filt_spec = forward_transform(filt[0].T, tables)
     grad_in = incoming.astype(jnp.float32)
     grad_mix = (grad_in * query).astype(jnp.bfloat16)
-    gated_part = lax.all_to_all(gated, "ctx", split_axis=1, concat_axis=0, tiled=True)
+    gated_part = jnp.concatenate(
+        lax.all_to_all(jnp.stack(jnp.split(gated, lax.axis_size("ctx"), axis=1)), "ctx", 0, 0),
+        axis=0,
+    )
     gated_f = gated_part.astype(jnp.float32)
     gated_spec = forward_transform(gated_part, tables)
     mixed = inverse_transform(cmul(gated_spec, filt_spec, False), tables)

time: 625 us -> 529 us (0.85)
  other arithmetic: 228 us -> 117 us
  waiting for transfers between devices: 160 us -> 206 us
  local copies, waits for them, and re-layouts: 72.4 us -> 44.7 us
    psum x1, waiting for transfers between devices: 68.2 us -> 108 us  [on_device(): lax.psum(partial_kern.astype(jnp.bfloat16), 'ctx').astype(jnp.float32)]
    unnamed x9 -> x10, other arithmetic: 52.6 us -> 19.7 us
    broadcast_in_dim x1, other arithmetic: 31.6 us -> 7.59 us  [on_device(): input_grad[None]]
    add x1, other arithmetic: 24.5 us -> 5.15 us  [on_device(): sum((weights[offset][None, :] * padded[margin - offset:margin - offset +...]
    concatenate x1, other arithmetic: 12.3 us -> 2.82 us  [on_device(): extended = jnp.concatenate([feat_grad, after], axis=0)]
    unnamed x84 -> x83, local copies, waits for them, and re-layouts: 19.6 us -> 10.2 us
    slice x2 -> x1, local copies, waits for them, and re-layouts: 7.43 us -> 0.97 us  [on_device(): before = from_behind(source[tokens_dev - margin:], 'ctx', 1)]
    concatenate x1, other arithmetic: 6.71 us -> 0.34 us  [on_device(): jnp.concatenate([grad_in * inner, through_f * value, through_f * keyed],...]
  transfers between devices with their start and end apart: 7 -> 7, of which waited for: 5 -> 5; matrix products, arithmetic and copies ran while one was open for 31% -> 15% of each run, Pallas kernels for 0% -> 0%
where the time goes in v1:
time: 529 us; the launch traced here: 520 us
  waiting for transfers between devices  206 us (39%)
  other arithmetic  117 us (22%)
  matrix products  74.6 us (14%)
  local copies, waits for them, and re-layouts  44.7 us (8%)
  blocking collectives  38.7 us (7%)
  starting transfers between devices  24.1 us (5%)
  between operations  15 us (3%)
    psum x1, waiting for transfers between devices, on_device(): lax.psum(partial_kern.astype(jnp.bfloat16), 'ctx').astype(jnp.float32)  108 us
    ppermute x2, waiting for transfers between devices, passed_along(): return lax.ppermute(value, axis, pairs)  87.7 us
    dot_general x9, matrix products, contract(): return jnp.einsum(form, table, values, precision=lax.Precision.HIGH)  63.6 us
    unnamed x10, other arithmetic  19.7 us
    all_to_all x1, blocking collectives, on_device(): lax.all_to_all(through_part, 'ctx', split_axis=0, concat_axis=1, tiled=True)  19.4 us
    all_to_all x1, blocking collectives, on_device(): lax.all_to_all(jnp.stack(jnp.split(gated, lax.axis_size('ctx'), axis=1)),...  19.3 us
    dot_general x3, local copies, waits for them, and re-layouts, contract(): return jnp.einsum(form, table, values, precision=lax.Precision.HIGH)  17.9 us
    reduce_sum x1, other arithmetic, on_device(): jnp.sum(jnp.stack([feat_grad * padded[margin - offset:margin - offset + t...  16 us
  transfers between devices with their start and end apart: 7, of which 5 were waited for; matrix products, arithmetic and copies ran while one was open for 15% of the time, Pallas kernels for 0%

profile of v1, /device:TPU:25, one launch (start us, length us, event | category | flops | bytes accessed | tf_op | source)
XLA Modules:
  0.0 520.1 jit_solution(9017665727570421674)
XLA Ops:
  7.2 5.9 %collective-permute-start.2 = (bf16[1,128,4096]{2,1,0:T(8,128)(2,1)}, bf16[1,128,4096]{2,1,0:T(8,128)(2,1)S(1)}, u32[]{:S(2)}, u32[]{:S(2)}) collective-permute-start(bf16[1,128,4096]{2,1,0:T(8,128)(2,1)} %param.6), channel_id=1, source_target_pairs={{0,112},{16,0},{32,16},{48,32},{64,48},{80,64},{96,80},{112,96},{1... | collective-permute-start | bytes 3145736 | tf_op jit(solution)/shard_map/ppermute | solution.py:11
  14.6 87.7 %collective-permute-done = bf16[1,128,12288]{2,1,0:T(8,128)(2,1)} collective-permute-done((bf16[1,128,12288]{2,1,0:T(8,128)(2,1)}, bf16[1,128,12288]{2,1,0:T(8,128)(2,1)}, u32[]{:S(2)}, u32[]{:S(2)}) %collective-permute-start) | collective-permute-done | bytes 3145760 | tf_op jit(solution)/shard_map/ppermute | solution.py:11
  103.3 2.7 collective-permute-start.1
  106.7 1.5 copy.49
  108.6 2.8 maximum_convert_fusion
  111.5 5.2 multiply_add_fusion
  116.6 2.7 copy-done.5
  119.3 1.3 fusion.50
  120.6 1.6 copy.57
  122.3 1.3 copy.58
  123.6 7.0 %all-to-all-start.2 = ((bf16[128,16,256]{2,0,1:T(8,128)(2,1)}), bf16[128,16,256]{2,0,1:T(8,128)(2,1)S(1)}, u32[]{:S(2)}, u32[]{:S(2)}) async-start(bf16[128,16,256]{2,0,1:T(8,128)(2,1)} %copy.58), calls=%async_computation.2 | async-start | bytes 2097152 | tf_op jit(solution)/shard_map/all_to_all | solution.py:144
  130.6 1.3 fusion.63
  131.9 4.6 convolution_add_fusion.1
  136.5 7.9 %all-to-all-done.2 = bf16[128,16,256]{2,0,1:T(8,128)(2,1)S(1)} async-done(((bf16[128,16,256]{2,0,1:T(8,128)(2,1)}), bf16[128,16,256]{2,0,1:T(8,128)(2,1)S(1)}, u32[]{:S(2)}, u32[]{:S(2)}) %all-to-all-start.2) | async-done | bytes 1048608 | tf_op jit(solution)/shard_map/all_to_all | solution.py:144
  144.4 1.3 fusion.60
  145.7 1.3 convolution_add_fusion
  148.1 7.0 %multiply_add_fusion.5 = (f32[1,64,64,256]{3,1,2,0:T(8,128)}, f32[1,64,64,256]{3,1,2,0:T(8,128)}, f32[1,64,64,256]{3,1,2,0:T(8,128)}, f32[1,64,64,256]{3,1,2,0:T(8,128)}) fusion(f32[2,64,64,256]{3,1,2,0:T(8,128)S(1)} %convolution_add_fusion, f32[64,64]{0,1:T(8,128)S(1)} %get-tuple-element.59, f32[64,64]{0,1:T(8,128)S(1)} %get-tuple-element.60, ...), kind=kLoop, calls=%fused_computation.68 | loop fusion | flops 12582912 | bytes 33587200 | tf_op jit(solution)/shard_map/add | solution.py:77
  155.1 4.2 maximum_bitcast_fusion.4
  159.7 3.0 maximum_bitcast_fusion.1
  162.7 8.5 %fusion.40 = f32[2,64,64,256]{3,2,0,1:T(8,128)S(1)} fusion(f32[2,64,64,256,1]{3,1,2,0,4:T(8,128)S(1)} %maximum_bitcast_fusion.4, f32[1,64,2,64]{3,1,2,0:T(8,128)S(1)} %get-tuple-element.52, f32[1,64,2,64]{3,1,2,0:T(8,128)S(1)} %get-tuple-element.55), kind=kOutput, calls=%fused_computation.83 | convolution fusion | flops 1610629120 | bytes 16842752 | tf_op jit(solution)/shard_map/pqsj,skjc->pkqc/dot_general | solution.py:58
  171.2 8.7 %fusion.37 = f32[2,64,64,256]{3,2,0,1:T(8,128)S(1)} fusion(f32[2,64,64,256,1]{3,1,2,0,4:T(8,128)S(1)} %maximum_bitcast_fusion.1, f32[1,64,2,64]{3,1,2,0:T(8,128)S(1)} %get-tuple-element.52, f32[1,64,2,64]{3,1,2,0:T(8,128)S(1)} %get-tuple-element.55), kind=kOutput, calls=%fused_computation.82 | convolution fusion | flops 1610629120 | bytes 16842752 | tf_op jit(solution)/shard_map/pqsj,skjc->pkqc/dot_general | solution.py:58
  180.0 3.9 multiply_add_fusion.4
  184.5 6.1 %fusion.44 = f32[64,256,2,64]{1,3,2,0:T(8,128)S(1)} fusion(f32[1,64,64,256]{3,2,0,1:T(8,128)} %get-tuple-element.18, f32[1,64,64,256]{3,2,0,1:T(8,128)S(1)} %get-tuple-element.17, f32[1,64,2,64]{3,1,2,0:T(8,128)S(1)} %get-tuple-element.56, f32[1,64,2,64]{3,1,2,0:T(8,128)S(1)} %get-tuple-element.51), kind=kOutput, calls=%fused_computation.85 | convolution fusion | flops 1612726272 | bytes 16842752 | tf_op jit(solution)/shard_map/pjsq,skqc->pkjc/dot_general | solution.py:58
  190.6 4.9 copy.136
  195.5 1.9 multiply_subtract_fusion.2
  197.4 3.1 bitcast_multiply_fusion.1
  202.1 19.4 %all_to_all.41 = bf16[16,128,256]{2,1,0:T(8,128)(2,1)S(1)} all-to-all(bf16[16,128,256]{2,1,0:T(8,128)(2,1)S(1)} %fusion.48), channel_id=1, replica_groups=mesh['section'=8,'ctx'=16] {'ctx'}, dimensions={0} | all-to-all | bytes 2097152 | tf_op jit(solution)/shard_map/all_to_all | solution.py:153
  221.7 1.8 copy.65
  223.5 2.9 copy.66
  226.4 4.7 slice_multiply_fusion.6
  231.4 19.3 %all_to_all.42 = bf16[16,128,256]{2,1,0:T(8,128)(2,1)S(1)} all-to-all(bf16[16,128,256]{2,1,0:T(8,128)(2,1)S(1)} %fusion.78), channel_id=1, replica_groups=mesh['section'=8,'ctx'=16] {'ctx'}, dimensions={0} | all-to-all | bytes 2097152 | tf_op jit(solution)/shard_map/all_to_all | solution.py:136
  250.7 1.3 fusion.66
  252.0 1.3 convolution_add_fusion.2
  253.3 1.5 multiply_add_fusion.9
  254.8 4.1 maximum_bitcast_fusion
  258.9 14.0 %fusion.34 = f32[2,64,64,256]{3,2,0,1:T(8,128)} fusion(f32[2,64,64,256,1]{3,1,2,0,4:T(8,128)} %maximum_bitcast_fusion, f32[1,64,2,64]{3,1,2,0:T(8,128)S(1)} %get-tuple-element.52, f32[1,64,2,64]{3,1,2,0:T(8,128)S(1)} %get-tuple-element.55), kind=kOutput, calls=%fused_computation.81 | convolution fusion | flops 1610629120 | bytes 16842752 | tf_op jit(solution)/shard_map/pqsj,skjc->pkqc/dot_general | solution.py:58
  272.8 11.9 %multiply_add_fusion.2 = (f32[1,64,64,256]{3,2,0,1:T(8,128)}, f32[1,64,64,256]{3,2,0,1:T(8,128)}, f32[1,64,64,256]{3,2,0,1:T(8,128)}, f32[1,64,64,256]{3,2,0,1:T(8,128)}) fusion(f32[2,64,64,256]{3,2,0,1:T(8,128)S(1)} %bitcast.270, f32[2,64,64,256]{3,2,0,1:T(8,128)} %fusion.34, f32[2,64,64,256]{3,2,0,1:T(8,128)} %copy-done.4), kind=kLoop, calls=%fused_computation.62 | loop fusion | flops 12582912 | bytes 41943040 | tf_op jit(solution)/shard_map/add | solution.py:86
  284.8 6.5 %fusion.45 = f32[64,256,2,64]{1,3,2,0:T(8,128)S(1)} fusion(f32[1,64,64,256]{3,2,0,1:T(8,128)} %get-tuple-element.33, f32[1,64,64,256]{3,2,0,1:T(8,128)} %get-tuple-element.34, f32[1,64,2,64]{3,1,2,0:T(8,128)S(1)} %get-tuple-element.56, f32[1,64,2,64]{3,1,2,0:T(8,128)S(1)} %get-tuple-element.51), kind=kOutput, calls=%fused_computation.86 | convolution fusion | flops 1612726272 | bytes 16842752 | tf_op jit(solution)/shard_map/pjsq,skqc->pkjc/dot_general | solution.py:58
  291.2 4.9 copy.137
  296.1 6.7 %fusion.43 = f32[64,256,2,64]{1,3,2,0:T(8,128)S(1)} fusion(f32[1,64,64,256]{3,2,0,1:T(8,128)} %get-tuple-element.16, f32[1,64,64,256]{3,2,0,1:T(8,128)} %get-tuple-element.15, f32[1,64,2,64]{3,1,2,0:T(8,128)S(1)} %get-tuple-element.56, f32[1,64,2,64]{3,1,2,0:T(8,128)S(1)} %get-tuple-element.51), kind=kOutput, calls=%fused_computation.84 | convolution fusion | flops 1612726272 | bytes 16842752 | tf_op jit(solution)/shard_map/pjsq,skqc->pkjc/dot_general | solution.py:58
  302.8 8.2 %copy.135 = f32[64,256,2,64]{1,0,3,2:T(8,128)} copy(f32[64,256,2,64]{1,3,2,0:T(8,128)S(1)} %fusion.43) | data formatting | bytes 16777216 | tf_op jit(solution)/shard_map/pjsq,skqc->pkjc/dot_general | solution.py:58
  310.9 7.7 %multiply_subtract_fusion = (f32[1,64,64,256]{3,1,2,0:T(8,128)}, f32[1,64,64,256]{3,1,2,0:T(8,128)}, f32[1,64,64,256]{3,1,2,0:T(8,128)S(1)}, f32[1,64,64,256]{3,1,2,0:T(8,128)}) fusion(f32[2,64,64,256]{3,1,2,0:T(8,128)} %bitcast.275, f32[64,64]{0,1:T(8,128)S(1)} %get-tuple-element.59, f32[64,64]{0,1:T(8,128)S(1)} %get-tuple-element.60, ...), kind=kLoop, calls=%fused_computation.60 | loop fusion | flops 12582912 | bytes 33587200 | tf_op jit(solution)/shard_map/sub | solution.py:99
  318.7 5.1 fusion.51
  323.8 1.6 copy.55
  325.4 6.6 %all-to-all-start.1 = ((bf16[16,128,256]{2,1,0:T(8,128)(2,1)}), bf16[16,128,256]{2,1,0:T(8,128)(2,1)}, u32[]{:S(2)}, u32[]{:S(2)}) async-start(bf16[16,128,256]{2,1,0:T(8,128)(2,1)} %bitcast.286), calls=%async_computation.1 | async-start | bytes 2097152 | tf_op jit(solution)/shard_map/all_to_all | solution.py:143
  332.0 5.1 bitcast_multiply_fusion
  337.1 2.5 copy.70
  339.6 2.9 copy.71
  342.5 2.1 fusion.49
  345.9 1.5 convert_bitcast_fusion.1
  347.7 3.3 convert_multiply_fusion.1
  352.1 3.0 bitcast_dynamic-update-slice_fusion.6
  355.2 1.9 collective-permute-start.3
  357.1 3.1 bitcast_dynamic-update-slice_fusion.5
  360.1 2.9 bitcast_dynamic-update-slice_fusion.4
  363.1 3.0 bitcast_dynamic-update-slice_fusion.3
  366.1 3.0 bitcast_dynamic-update-slice_fusion.2
  369.2 3.1 bitcast_dynamic-update-slice_fusion.1
  372.3 3.0 bitcast_dynamic-update-slice_fusion
  375.3 16.0 %reduce_sum.18 = bf16[7,12288]{1,0:T(8,128)(2,1)S(1)} reduce(f32[7,128,12288]{2,1,0:T(8,128)} %bitcast_dynamic-update-slice_fusion, f32[]{:T(128)} %constant.55.clone.1), dimensions={1}, to_apply=%region_0.1 | reduce | flops 10924032 | bytes 44212228 | tf_op jit(solution)/shard_map/reduce_sum | solution.py:166
  392.3 2.8 pad_maximum_fusion
  395.2 7.6 %fusion.46 = bf16[1,128,12288]{2,1,0:T(8,128)(2,1)} fusion(f32[134,12288]{1,0:T(8,128)S(1)} %pad_maximum_fusion, f32[12288]{0:T(1024)S(1)} %bitcast.299, f32[12288]{0:T(1024)S(1)} %bitcast.301, f32[12288]{0:T(1024)S(1)} %bitcast.291, f32[12288]{0:T(1024)S(1)} %bitcast.293, f32[12288]{0:T(1024)S(1)} %bitcast.295, f32[12288]{0:T(1024)S(1)} %bitcast.297, ...), kind=kLoop, calls=%fused_computation.87 | loop fusion | flops 25165824 | bytes 47529984 | tf_op jit(solution)/shard_map/broadcast_in_dim | solution.py:177
  402.8 108.2 %all-reduce.2.cloned.1.call-done = bf16[1,7,12288]{2,0,1:T(2,128)(2,1)} async-done(((bf16[1,7,12288]{2,0,1:T(2,128)(2,1)}), bf16[1,7,12288]{2,0,1:T(2,128)(2,1)}) %all-reduce.2.cloned.1.call-update) | async-done | bytes 172048 | tf_op jit(solution)/shard_map/psum | solution.py:176
  511.0 2.1 broadcast_in_dim.16
  (107 shorter events, 11.3 us)
Async XLA Ops:
  7.2 109.5 %collective-permute-start.2 = (bf16[1,128,4096]{2,1,0:T(8,128)(2,1)}, bf16[1,128,4096]{2,1,0:T(8,128)(2,1)S(1)}, u32[]{:S(2)}, u32[]{:S(2)}) collective-permute-start(bf16[1,128,4096]{2,1,0:T(8,128)(2,1)} %param.6), channel_id=1, source_target_pairs={{0,112},{16,0},{32,16},{48,32},{64,48},{80,64},{96,80},{112,96},{1... | collective-permute-start | bytes 3145736 | tf_op jit(solution)/shard_map/ppermute | solution.py:11
  13.0 89.3 %collective-permute-start = (bf16[1,128,12288]{2,1,0:T(8,128)(2,1)}, bf16[1,128,12288]{2,1,0:T(8,128)(2,1)}, u32[]{:S(2)}, u32[]{:S(2)}) collective-permute-start(bf16[1,128,12288]{2,1,0:T(8,128)(2,1)} %param.5), channel_id=1, source_target_pairs={{0,16},{16,32},{32,48},{48,64},{64,80},{80,96},{96,112},{112,0},{1... | collective-permute-start | bytes 9437192 | tf_op jit(solution)/shard_map/ppermute | solution.py:11
  14.5 96.9 %copy-start.12 = (f32[1,1,12288]{2,0,1:T(1,128)}, f32[1,1,12288]{2,0,1:T(1,128)S(1)}, u32[]{:S(2)}) copy-start(f32[1,1,12288]{2,0,1:T(1,128)S(1)} %get-tuple-element.40) | copy-start | bytes 147460
  14.5 96.9 %copy-start.14 = (f32[1,1,12288]{2,0,1:T(1,128)}, f32[1,1,12288]{2,0,1:T(1,128)S(1)}, u32[]{:S(2)}) copy-start(f32[1,1,12288]{2,0,1:T(1,128)S(1)} %get-tuple-element.41) | copy-start | bytes 147460
  14.6 96.9 %copy-start.16 = (f32[1,1,12288]{2,0,1:T(1,128)}, f32[1,1,12288]{2,0,1:T(1,128)S(1)}, u32[]{:S(2)}) copy-start(f32[1,1,12288]{2,0,1:T(1,128)S(1)} %get-tuple-element.42) | copy-start | bytes 147460
  14.6 96.9 %copy-start.18 = (f32[1,1,12288]{2,0,1:T(1,128)}, f32[1,1,12288]{2,0,1:T(1,128)S(1)}, u32[]{:S(2)}) copy-start(f32[1,1,12288]{2,0,1:T(1,128)S(1)} %get-tuple-element.43) | copy-start | bytes 147460
  14.6 96.9 %copy-start.20 = (f32[1,1,12288]{2,0,1:T(1,128)}, f32[1,1,12288]{2,0,1:T(1,128)S(1)}, u32[]{:S(2)}) copy-start(f32[1,1,12288]{2,0,1:T(1,128)S(1)} %get-tuple-element.44) | copy-start | bytes 147460
  14.6 96.9 %copy-start.22 = (f32[1,1,12288]{2,0,1:T(1,128)}, f32[1,1,12288]{2,0,1:T(1,128)S(1)}, u32[]{:S(2)}) copy-start(f32[1,1,12288]{2,0,1:T(1,128)S(1)} %get-tuple-element.45) | copy-start | bytes 147460
  14.6 96.9 %copy-start.24 = (f32[1,1,12288]{2,0,1:T(1,128)}, f32[1,1,12288]{2,0,1:T(1,128)S(1)}, u32[]{:S(2)}) copy-start(f32[1,1,12288]{2,0,1:T(1,128)S(1)} %get-tuple-element.46) | copy-start | bytes 147460
  103.3 5.3 %collective-permute-start.1 = (bf16[6,12288]{1,0:T(8,128)(2,1)S(1)}, bf16[6,12288]{1,0:T(8,128)(2,1)S(1)}, u32[]{:S(2)}, u32[]{:S(2)}) collective-permute-start(bf16[6,12288]{1,0:T(8,128)(2,1)S(1)} %slice_bitcast_fusion), channel_id=1, source_target_pairs={{0,1},{1,2},{2,3},{3,4},{4,5},{5,6},{6,7},{7,8},{8,9},{9,10},{10,1... | collective-permute-start | bytes 442376 | tf_op jit(solution)/shard_map/ppermute | solution.py:17
  111.4 5.2 %copy-start = (f32[134,12288]{1,0:T(8,128)}, f32[134,12288]{1,0:T(8,128)S(1)}, u32[]{:S(2)}) copy-start(f32[134,12288]{1,0:T(8,128)S(1)} %maximum_convert_fusion) | copy-start | bytes 19759108
  116.6 2.7 copy-start.5
  119.3 12.5 %copy-start.10 = (bf16[1,128,4096]{2,1,0:T(8,128)(2,1)}, bf16[1,128,4096]{2,1,0:T(8,128)(2,1)S(1)}, u32[]{:S(2)}) copy-start(bf16[1,128,4096]{2,1,0:T(8,128)(2,1)S(1)} %collective-permute-done.2) | copy-start | bytes 3145732
  123.6 20.8 %all-to-all-start.2 = ((bf16[128,16,256]{2,0,1:T(8,128)(2,1)}), bf16[128,16,256]{2,0,1:T(8,128)(2,1)S(1)}, u32[]{:S(2)}, u32[]{:S(2)}) async-start(bf16[128,16,256]{2,0,1:T(8,128)(2,1)} %copy.58), calls=%async_computation.2 | async-start | bytes 2097152 | tf_op jit(solution)/shard_map/all_to_all | solution.py:144
  144.4 2.6 slice-start.4
  145.7 2.4 slice-start.5
  155.0 4.6 copy-start.7
  171.2 8.7 %copy-start.3 = (f32[2,64,64,256]{3,2,0,1:T(8,128)}, f32[2,64,64,256]{3,2,0,1:T(8,128)S(1)}, u32[]{:S(2)}) copy-start(f32[2,64,64,256]{3,2,0,1:T(8,128)S(1)} %fusion.40) | copy-start | bytes 25165828
  179.9 4.6 copy-start.4
  231.1 19.6 %copy-start.8 = (bf16[128,4096]{1,0:T(8,128)(2,1)}, bf16[128,4096]{1,0:T(8,128)(2,1)S(1)}, u32[]{:S(2)}) copy-start(bf16[128,4096]{1,0:T(8,128)(2,1)S(1)} %get-tuple-element.37) | copy-start | bytes 3145732
  250.7 2.6 copy-start.6
  254.7 18.1 %slice-start.2 = ((s8[8388608]{0:T(1024)(128)(4,1)}), s8[4194304]{0:T(1024)(128)(4,1)S(1)}, s32[]{:S(2)}) async-start(s8[8388608]{0:T(1024)(128)(4,1)} %bitcast.269), calls=%async_computation.7 | async-start | bytes 8388608
  258.9 14.0 %slice-start.3 = ((s8[8388608]{0:T(1024)(128)(4,1)}), s8[4194304]{0:T(1024)(128)(4,1)S(1)}, s32[]{:S(2)}) async-start(s8[8388608]{0:T(1024)(128)(4,1)} %bitcast.269), calls=%async_computation.8 | async-start | bytes 8388608
  325.4 20.6 %all-to-all-start.1 = ((bf16[16,128,256]{2,1,0:T(8,128)(2,1)}), bf16[16,128,256]{2,1,0:T(8,128)(2,1)}, u32[]{:S(2)}, u32[]{:S(2)}) async-start(bf16[16,128,256]{2,1,0:T(8,128)(2,1)} %bitcast.286), calls=%async_computation.1 | async-start | bytes 2097152 | tf_op jit(solution)/shard_map/all_to_all | solution.py:143
  332.0 179.0 %all-reduce.2.cloned.1.call-start = ((), (), s32[]{:S(2)}) async-start(), calls=%async_computation.4 | async-start | bytes 688128 | tf_op jit(solution)/shard_map/psum | solution.py:176
  339.6 8.1 %copy-start.26 = (f32[1,4096]{1,0:T(1,128)S(1)}, f32[1,4096]{1,0:T(1,128)}, u32[]{:S(2)}) copy-start(f32[1,4096]{1,0:T(1,128)} %param.9) | copy-start | bytes 49156
  344.7 3.1 copy-start.9
  345.9 1.8 copy-start.11
  347.5 3.6 copy-start.1
  347.7 3.7 slice-start
  347.7 4.4 slice-start.1
  351.0 21.2 %copy-start.2 = (f32[128,4096]{1,0:T(8,128)}, f32[128,4096]{1,0:T(8,128)S(1)}, u32[]{:S(2)}) copy-start(f32[128,4096]{1,0:T(8,128)S(1)} %get-tuple-element.38) | copy-start | bytes 6291460
  355.2 37.0 %collective-permute-start.3 = (bf16[6,12288]{1,0:T(8,128)(2,1)S(1)}, bf16[6,12288]{1,0:T(8,128)(2,1)S(1)}, u32[]{:S(2)}, u32[]{:S(2)}) collective-permute-start(bf16[6,12288]{1,0:T(8,128)(2,1)S(1)} %slice.372), channel_id=1, source_target_pairs={{1,0},{2,1},{3,2},{4,3},{5,4},{6,5},{7,6},{8,7},{9,8},{10,9},{11,1... | collective-permute-start | bytes 442376 | tf_op jit(solution)/shard_map/ppermute | solution.py:17
  392.2 2.9 copy-start.13
  392.2 2.9 copy-start.15
  392.3 2.9 copy-start.17
  392.3 2.9 copy-start.19
  392.3 2.9 copy-start.21
  392.3 2.9 copy-start.23
  392.3 2.9 copy-start.25
Sparse Core Ops, SparseCore 0:
  392.3 118.6 all-reduce.1
